TPU v7x, 256 devices: a whole 4x4x8 slice. The times are simulated.
256 devices in a mesh: dp: 16 (over x, y), head: 16 (over z, core).
Axes of the slice: x: 4, y: 4, z: 8, core: 2. Of those that a mesh axis runs over, the one named last changes fastest.
Arguments:
- latents: bfloat16 [2048, 512], P('dp'), may hold values from -6 to 6
- targets: bfloat16 [2048, 32768], P('dp', 'head'), may hold values from -6 to 6
- kv_weight: bfloat16 [512, 32768], P(None, 'head'), may hold values from -0.25 to 0.25
- momentum: float32 [512, 16, 2048], P(None, 'head', 'dp'), may hold values from -120 to 120
Outputs:
- momentum_out: float32 [512, 16, 2048], P(None, 'head', 'dp')
- update: float32 [512, 16, 2048], P(None, 'head', 'dp')
All inputs are finite; a program needn't handle non-finite values.
Results may differ from a plain program's by a relative error of at most 0.0003.
The roundings to bfloat16 on the way count: a program that leaves them out, or rounds other values in their place, can miss the bound.
Values may be sent and summed in bfloat16 or wider, within the bound.
A program may use at most 64 MiB of HBM per device.

v0:
```python
import math
import jax
import jax.numpy as jnp
from jax import lax
from jax.sharding import PartitionSpec as P

C = 32768
decay_rate = 0.95
linear_coef = 3.4445
square_coef = -4.775
quint_coef = 2.0315
epsilon = 1e-07
HIGHEST = lax.Precision.HIGHEST


def local(latents, targets, kv_weight, momentum):
    latent_width = momentum.shape[0]
    sub_width = momentum.shape[2]
    total_tokens = latents.shape[0] * lax.axis_size("dp")
    all_latents = lax.all_gather(latents, "dp", axis=0, tiled=True)
    my_targets = lax.all_to_all(targets, "dp", split_axis=1, concat_axis=0, tiled=True)
    start = lax.axis_index("dp") * sub_width
    my_weight = lax.dynamic_slice(kv_weight, (0, start), (latent_width, sub_width))
    residual = (
        jnp.dot(all_latents, my_weight, preferred_element_type=jnp.float32)
        - my_targets.astype(jnp.float32)
    ).astype(jnp.bfloat16)
    gradient = lax.dot_general(
        all_latents, residual, (((0,), (0,)), ((), ())), preferred_element_type=jnp.float32
    ) * (1.0 / math.sqrt(total_tokens))
    momentum_new = decay_rate * momentum.reshape(latent_width, sub_width) + gradient
    nesterov = gradient + decay_rate * momentum_new
    gram = lax.psum(
        lax.dot_general(nesterov, nesterov, (((1,), (1,)), ((), ())), precision=HIGHEST),
        ("dp", "head"),
    )
    inverse = 1.0 / (jnp.sqrt(jnp.trace(gram)) + epsilon)
    gram = gram * (inverse * inverse)
    eye = jnp.eye(latent_width, dtype=jnp.float32)
    first = (
        linear_coef * eye + square_coef * gram + quint_coef * jnp.dot(gram, gram, precision=HIGHEST)
    )
    second_gram = jnp.dot(first, jnp.dot(gram, first, precision=HIGHEST), precision=HIGHEST)
    second = (
        linear_coef * eye
        + square_coef * second_gram
        + quint_coef * jnp.dot(second_gram, second_gram, precision=HIGHEST)
    )
    iterate = jnp.dot(first, nesterov * (inverse * math.sqrt(C)), precision=HIGHEST)
    update = jnp.dot(second, iterate, precision=HIGHEST)
    return (
        momentum_new.reshape(latent_width, 1, sub_width),
        update.reshape(latent_width, 1, sub_width),
    )


def solution(mesh):
    return jax.shard_map(
        local,
        mesh=mesh,
        in_specs=(P("dp", None), P("dp", "head"), P(None, "head"), P(None, "head", "dp")),
        out_specs=(P(None, "head", "dp"), P(None, "head", "dp")),
        check_vma=False,
    )
```

profile of v0, /device:TPU:2, one launch (start us, length us, event | category | flops | bytes accessed | tf_op | source)
XLA Modules:
  0.0 346.6 jit_solution(12459691134939242747)
XLA Ops:
  7.2 0.0 copy-start
  7.2 0.0 copy-start.2
  7.2 0.0 all-gather.2.cloned.1.call-start
  7.2 0.7 all-gather.2.cloned.1.call-update
  7.9 2.0 copy.13
  10.0 7.5 %all-to-all-start = ((bf16[128,16,128]{0,2,1:T(8,128)(2,1)}), bf16[128,16,128]{0,2,1:T(8,128)(2,1)}, u32[]{:S(2)}, u32[]{:S(2)}) async-start(bf16[128,16,128]{0,2,1:T(8,128)(2,1)} %bitcast.2), calls=%async_computation | async-start | bytes 1048576 | tf_op jit(solution)/shard_map/all_to_all | solution.py:21
  17.5 0.0 all-reduce.2.cloned.1.call-start
  17.5 0.0 copy-done.2
  17.5 0.1 copy.12
  17.6 9.2 %all-to-all-done = bf16[128,16,128]{0,2,1:T(8,128)(2,1)} async-done(((bf16[128,16,128]{0,2,1:T(8,128)(2,1)}), bf16[128,16,128]{0,2,1:T(8,128)(2,1)}, u32[]{:S(2)}, u32[]{:S(2)}) %all-to-all-start) | async-done | bytes 524320 | tf_op jit(solution)/shard_map/all_to_all | solution.py:21
  26.9 1.1 convert_bitcast_fusion
  28.0 1.3 copy.14
  29.3 2.6 copy.15
  31.9 31.2 %all-gather.2.cloned.1.call-done = bf16[2048,512]{1,0:T(8,128)(2,1)} async-done(((bf16[128,512]{1,0:T(8,128)(2,1)}), bf16[2048,512]{1,0:T(8,128)(2,1)}) %all-gather.2.cloned.1.call-update) | async-done | bytes 2097168 | tf_op jit(solution)/shard_map/all_gather | solution.py:20
  63.1 0.0 copy-done
  63.1 3.7 %fusion.6 = f32[512,128]{0,1:T(8,128)S(1)} fusion(bf16[2048,512]{1,0:T(8,128)(2,1)} %all-gather.2.cloned.1.call-done, f32[2048,128]{0,1:T(8,128)} %copy.15, bf16[512,2048]{1,0:T(8,128)(2,1)S(1)} %copy-done, s32[]{:T(128)S(6)} %select_n.8), kind=kOutput, calls=%fused_computation.11 | convolution fusion | flops 537460736 | bytes 5636100 | tf_op jit(solution)/shard_map/dot_general | solution.py:28
  66.7 2.1 fusion.18
  68.8 0.0 all-reduce.2.cloned.1.call-update
  68.9 0.8 copy.16
  69.7 255.0 %all-reduce.2.cloned.1.call-done = f32[512,512]{1,0:T(8,128)} async-done(((f32[512,512]{1,0:T(8,128)}), f32[512,512]{1,0:T(8,128)}) %all-reduce.2.cloned.1.call-update) | async-done | bytes 1048592 | tf_op jit(solution)/shard_map/psum | solution.py:33
  324.7 1.9 select_reduce_fusion
  327.3 0.0 copy-start.1
  327.4 4.1 %fusion.3 = f32[512,512]{1,0:T(8,128)S(1)} fusion(f32[512,512]{1,0:T(8,128)} %all-reduce.2.cloned.1.call-done, f32[]{:T(128)S(6)} %mul.65), kind=kOutput, calls=%fused_computation.8 | convolution fusion | flops 1612709888 | bytes 2097156 | tf_op jit(solution)/shard_map/dot_general | solution.py:41
  331.4 1.0 fusion.12
  332.4 0.0 copy-done.1
  332.4 1.9 fusion.8
  334.3 1.8 fusion.23
  336.2 1.9 fusion.2
  338.1 1.7 fusion.24
  (1 shorter events, 0.0 us)
Async XLA Ops:
  7.2 55.9 %copy-start = (bf16[512,2048]{1,0:T(8,128)(2,1)S(1)}, bf16[512,2048]{1,0:T(8,128)(2,1)}, u32[]{:S(2)}) copy-start(bf16[512,2048]{1,0:T(8,128)(2,1)} %param.6) | copy-start | bytes 6291460
  7.2 10.3 %copy-start.2 = (f32[512,1,128]{2,1,0:T(1,128)S(1)}, f32[512,1,128]{2,1,0:T(1,128)}, u32[]{:S(2)}) copy-start(f32[512,1,128]{2,1,0:T(1,128)} %param.7) | copy-start | bytes 786436
  7.2 55.9 %all-gather.2.cloned.1.call-start = ((), (), s32[]{:S(2)}) async-start(), calls=%async_computation.1 | async-start | bytes 2228224 | tf_op jit(solution)/shard_map/all_gather | solution.py:20
  10.0 16.9 %all-to-all-start = ((bf16[128,16,128]{0,2,1:T(8,128)(2,1)}), bf16[128,16,128]{0,2,1:T(8,128)(2,1)}, u32[]{:S(2)}, u32[]{:S(2)}) async-start(bf16[128,16,128]{0,2,1:T(8,128)(2,1)} %bitcast.2), calls=%async_computation | async-start | bytes 1048576 | tf_op jit(solution)/shard_map/all_to_all | solution.py:21
  17.5 307.3 %all-reduce.2.cloned.1.call-start = ((), (), s32[]{:S(2)}) async-start(), calls=%async_computation.2 | async-start | bytes 2097152 | tf_op jit(solution)/shard_map/psum | solution.py:33
  327.3 5.1 %copy-start.1 = (f32[512,512]{1,0:T(8,128)S(1)}, f32[512,512]{1,0:T(8,128)}, u32[]{:S(2)}) copy-start(f32[512,512]{1,0:T(8,128)} %all-reduce.2.cloned.1.call-done) | copy-start | bytes 3145732
Sparse Core Ops, SparseCore 0:
  10.5 52.5 all-gather.1
  68.9 255.7 all-reduce.1
where the time goes:
time: 347 us
  waiting for transfers between devices  296 us (85%)
  matrix products  18.1 us (5%)
  between operations  14.9 us (4%)
  starting transfers between devices  7.55 us (2%)
  local copies, waits for them, and re-layouts  6.9 us (2%)
    psum x1, waiting for transfers between devices, local(): lax.psum(lax.dot_general(nesterov, nesterov, (((1,), (1,)), ((), ())), pr...  255 us
    all_gather x1, waiting for transfers between devices, local(): all_latents = lax.all_gather(latents, 'dp', axis=0, tiled=True)  31.2 us
    all_to_all x1, waiting for transfers between devices, local(): lax.all_to_all(targets, 'dp', split_axis=1, concat_axis=0, tiled=True)  9.24 us
    all_to_all x1, starting transfers between devices, local(): lax.all_to_all(targets, 'dp', split_axis=1, concat_axis=0, tiled=True)  7.48 us
  transfers between devices with their start and end apart: 3, of which 3 were waited for; matrix products, arithmetic and copies ran while one was open for 2% of the time, Pallas kernels for 0%

commit v1 on v0

--- a/solution.py
+++ b/solution.py
@@ -31,8 +31,10 @@
     momentum_new = decay_rate * momentum.reshape(latent_width, sub_width) + gradient
     nesterov = gradient + decay_rate * momentum_new
     gram = lax.psum(
-        lax.dot_general(nesterov, nesterov, (((1,), (1,)), ((), ())), precision=HIGHEST),
-        ("dp", "head"),
+        lax.psum(
+            lax.dot_general(nesterov, nesterov, (((1,), (1,)), ((), ())), precision=HIGHEST), "head"
+        ),
+        "dp",
     )
     inverse = 1.0 / (jnp.sqrt(jnp.trace(gram)) + epsilon)
     gram = gram * (inverse * inverse)

time: 347 us -> 305 us (0.88)
  waiting for transfers between devices: 296 us -> 252 us
    psum x1, waiting for transfers between devices: 255 us -> 111 us  [local(): lax.psum(lax.dot_general(nesterov, nesterov, (((1,), (1,)), ((), ())), pr...]
    psum x0 -> x1, waiting for transfers between devices: none -> 99.6 us  [local(): lax.psum(lax.psum(lax.dot_general(nesterov, nesterov, (((1,), (1,)), ((),...]
  transfers between devices with their start and end apart: 3 -> 4, of which waited for: 3 -> 4; matrix products, arithmetic and copies ran while one was open for 2% -> 3% of each run, Pallas kernels for 0% -> 0%
where the time goes in v1:
time: 305 us; the launch traced here: 304 us
  waiting for transfers between devices  252 us (83%)
  matrix products  20 us (7%)
  between operations  14.6 us (5%)
  starting transfers between devices  7.78 us (3%)
  local copies, waits for them, and re-layouts  6.92 us (2%)
  other arithmetic  3.13 us (1%)
    psum x1, waiting for transfers between devices, local(): lax.psum(lax.dot_general(nesterov, nesterov, (((1,), (1,)), ((), ())), pr...  111 us
    psum x1, waiting for transfers between devices, local(): lax.psum(lax.psum(lax.dot_general(nesterov, nesterov, (((1,), (1,)), ((),...  99.6 us
    all_gather x1, waiting for transfers between devices, local(): all_latents = lax.all_gather(latents, 'dp', axis=0, tiled=True)  31.2 us
    all_to_all x1, waiting for transfers between devices, local(): lax.all_to_all(targets, 'dp', split_axis=1, concat_axis=0, tiled=True)  9.22 us
    all_to_all x1, starting transfers between devices, local(): lax.all_to_all(targets, 'dp', split_axis=1, concat_axis=0, tiled=True)  7.48 us
  transfers between devices with their start and end apart: 4, of which 4 were waited for; matrix products, arithmetic and copies ran while one was open for 3% of the time, Pallas kernels for 0%

profile of v1, /device:TPU:2, one launch (start us, length us, event | category | flops | bytes accessed | tf_op | source)
XLA Modules:
  0.0 304.4 jit_solution(3524235866132822471)
XLA Ops:
  7.2 0.0 copy-start
  7.2 0.0 copy-start.4
  7.2 0.0 all-gather.2.cloned.1.call-start
  7.2 0.7 all-gather.2.cloned.1.call-update
  7.9 2.1 copy.13
  10.0 7.5 %all-to-all-start = ((bf16[128,16,128]{0,2,1:T(8,128)(2,1)}), bf16[128,16,128]{0,2,1:T(8,128)(2,1)}, u32[]{:S(2)}, u32[]{:S(2)}) async-start(bf16[128,16,128]{0,2,1:T(8,128)(2,1)} %bitcast.2), calls=%async_computation | async-start | bytes 1048576 | tf_op jit(solution)/shard_map/all_to_all | solution.py:21
  17.5 0.0 all-reduce.3.cloned.1.call-start
  17.5 0.0 copy-done.4
  17.5 0.1 copy.12
  17.7 0.0 copy-start.3
  17.7 9.2 %all-to-all-done = bf16[128,16,128]{0,2,1:T(8,128)(2,1)} async-done(((bf16[128,16,128]{0,2,1:T(8,128)(2,1)}), bf16[128,16,128]{0,2,1:T(8,128)(2,1)}, u32[]{:S(2)}, u32[]{:S(2)}) %all-to-all-start) | async-done | bytes 524320 | tf_op jit(solution)/shard_map/all_to_all | solution.py:21
  26.9 1.1 convert_bitcast_fusion
  28.0 1.3 copy.14
  29.4 2.5 copy.15
  31.9 31.2 %all-gather.2.cloned.1.call-done = bf16[2048,512]{1,0:T(8,128)(2,1)} async-done(((bf16[128,512]{1,0:T(8,128)(2,1)}), bf16[2048,512]{1,0:T(8,128)(2,1)}) %all-gather.2.cloned.1.call-update) | async-done | bytes 2097168 | tf_op jit(solution)/shard_map/all_gather | solution.py:20
  63.1 0.0 copy-done
  63.1 3.7 %fusion.6 = f32[512,128]{0,1:T(8,128)S(1)} fusion(bf16[2048,512]{1,0:T(8,128)(2,1)} %all-gather.2.cloned.1.call-done, f32[2048,128]{0,1:T(8,128)} %copy.15, bf16[512,2048]{1,0:T(8,128)(2,1)S(1)} %copy-done, s32[]{:T(128)S(6)} %select_n.8), kind=kOutput, calls=%fused_computation.11 | convolution fusion | flops 537460736 | bytes 5636100 | tf_op jit(solution)/shard_map/dot_general | solution.py:28
  66.7 2.0 fusion.18
  68.8 0.0 all-reduce.3.cloned.1.call-update
  68.8 0.2 all-reduce.5.cloned.1.call-start
  69.0 111.2 %all-reduce.3.cloned.1.call-done = f32[512,512]{1,0:T(8,128)} async-done(((f32[512,512]{1,0:T(8,128)}), f32[512,512]{1,0:T(8,128)}) %all-reduce.3.cloned.1.call-update) | async-done | bytes 1048592 | tf_op jit(solution)/shard_map/psum | solution.py:34
  180.2 0.0 all-reduce.5.cloned.1.call-update
  180.2 0.0 copy-done.3
  180.3 0.8 copy.16
  181.1 99.6 %all-reduce.5.cloned.1.call-done = f32[512,512]{1,0:T(8,128)} async-done(((f32[512,512]{1,0:T(8,128)}), f32[512,512]{1,0:T(8,128)}) %all-reduce.5.cloned.1.call-update) | async-done | bytes 1048592 | tf_op jit(solution)/shard_map/psum | solution.py:33
  280.7 2.0 select_reduce_fusion
  283.4 0.0 copy-start.2
  283.4 4.1 %fusion.3 = f32[512,512]{1,0:T(8,128)S(1)} fusion(f32[512,512]{1,0:T(8,128)} %all-reduce.5.cloned.1.call-done, f32[]{:T(128)S(6)} %mul.65), kind=kOutput, calls=%fused_computation.8 | convolution fusion | flops 1612709888 | bytes 2097156 | tf_op jit(solution)/shard_map/dot_general | solution.py:43
  287.5 0.0 copy-done.2
  287.5 1.9 fusion.8
  289.4 1.8 fusion.23
  291.2 2.9 fusion.2
  294.1 0.0 copy-start.1
  294.1 2.0 fusion.12
  296.1 0.0 copy-done.1
  296.1 1.7 fusion.24
  (1 shorter events, 0.0 us)
Async XLA Ops:
  7.2 55.9 %copy-start = (bf16[512,2048]{1,0:T(8,128)(2,1)S(1)}, bf16[512,2048]{1,0:T(8,128)(2,1)}, u32[]{:S(2)}) copy-start(bf16[512,2048]{1,0:T(8,128)(2,1)} %param.6) | copy-start | bytes 6291460
  7.2 10.3 %copy-start.4 = (f32[512,1,128]{2,1,0:T(1,128)S(1)}, f32[512,1,128]{2,1,0:T(1,128)}, u32[]{:S(2)}) copy-start(f32[512,1,128]{2,1,0:T(1,128)} %param.7) | copy-start | bytes 786436
  7.2 55.9 %all-gather.2.cloned.1.call-start = ((), (), s32[]{:S(2)}) async-start(), calls=%async_computation.1 | async-start | bytes 2228224 | tf_op jit(solution)/shard_map/all_gather | solution.py:20
  10.0 16.9 %all-to-all-start = ((bf16[128,16,128]{0,2,1:T(8,128)(2,1)}), bf16[128,16,128]{0,2,1:T(8,128)(2,1)}, u32[]{:S(2)}, u32[]{:S(2)}) async-start(bf16[128,16,128]{0,2,1:T(8,128)(2,1)} %bitcast.2), calls=%async_computation | async-start | bytes 1048576 | tf_op jit(solution)/shard_map/all_to_all | solution.py:21
  17.5 162.7 %all-reduce.3.cloned.1.call-start = ((), (), s32[]{:S(2)}) async-start(), calls=%async_computation.2 | async-start | bytes 2097152 | tf_op jit(solution)/shard_map/psum | solution.py:34
  17.7 162.6 %copy-start.3 = (f32[512,1,128]{0,2,1:T(8,128)}, f32[512,1,128]{0,2,1:T(8,128)S(1)}, u32[]{:S(2)}) copy-start(f32[512,1,128]{0,2,1:T(8,128)S(1)} %copy.12) | copy-start | bytes 786436
  68.8 212.0 %all-reduce.5.cloned.1.call-start = ((), (), s32[]{:S(2)}) async-start(), calls=%async_computation.3 | async-start | bytes 2097152 | tf_op jit(solution)/shard_map/psum | solution.py:33
  283.4 4.1 %copy-start.2 = (f32[512,512]{1,0:T(8,128)S(1)}, f32[512,512]{1,0:T(8,128)}, u32[]{:S(2)}) copy-start(f32[512,512]{1,0:T(8,128)} %all-reduce.5.cloned.1.call-done) | copy-start | bytes 3145732
  294.1 2.0 copy-start.1
Sparse Core Ops, SparseCore 0:
  10.5 52.5 all-gather.1
  68.9 111.2 all-reduce.2
  183.8 96.9 all-reduce.4
